TPU v7x, 32 devices: a whole 2x2x4 slice. The times are simulated.
32 devices in a mesh: kpool: 8 (over y, x, core), band: 4 (over z).
Axes of the slice: x: 2, y: 2, z: 4, core: 2. Of those that a mesh axis runs over, the one named last changes fastest.
Arguments:
- psi: bfloat16 [8, 2, 4, 48, 2304], P('kpool', None, 'band'), may hold values from -6 to 6
- kpoint_of_pool: int32 [8], replicated, may hold values from 0 to 7, each once
Outputs:
- exchange: float32 [8, 2, 4, 48, 2304], P('kpool', None, 'band')
Inputs may be any that keep to these rules, and one draw needn't show every extreme that they name: `kpoint_of_pool`: each value appears once.
All inputs are finite; a program needn't handle non-finite values.
Results may differ from a plain program's by a relative error of at most 0.0003.
Values may be sent and summed in bfloat16 or wider, within the bound.
A program may use at most 64 MiB of HBM per device.

v0:
```python
import math

import jax
import jax.numpy as jnp
from jax import lax
from jax.sharding import PartitionSpec as P

GRID = 48
KMESH = 4
ROUNDS = 1


def passed_along(value, axis, by):
    size = lax.axis_size(axis)
    return lax.ppermute(value, axis, [(i, (i + by) % size) for i in range(size)])


def kpoint_coords(labels):
    first = labels % KMESH
    second = labels // KMESH % KMESH
    third = labels // (KMESH * KMESH)
    return jnp.stack([first, second, third], axis=1).astype(jnp.float32) / KMESH


def coulomb(offset):
    index = jnp.arange(GRID, dtype=jnp.int32)
    freq = jnp.where(index < GRID // 2, index, index - GRID).astype(jnp.float32)
    edge = index == GRID // 2
    along_x = (offset[0] + freq) ** 2
    along_y = (offset[1] + freq) ** 2
    along_z = (offset[2] + freq) ** 2
    squared = along_x[:, None, None] + along_y[None, :, None] + along_z[None, None, :]
    cutoff = edge[:, None, None] | edge[None, :, None] | edge[None, None, :]
    safe = jnp.where(cutoff, 1.0, squared)
    amplitude = GRID**1.5 / 16.0
    kernel = jnp.where(cutoff, 0.0, amplitude / safe)
    return kernel.reshape(GRID, GRID * GRID) / (GRID * GRID * GRID)


def stacked_table(cosine, sine):
    upper = jnp.concatenate([cosine, -sine], axis=1)
    lower = jnp.concatenate([sine, cosine], axis=1)
    return jnp.concatenate([upper, lower], axis=0)


def dft_tables():
    index = jnp.arange(GRID, dtype=jnp.int32)
    product = index[:, None] * index[None, :] % GRID
    angles = product.astype(jnp.float32) * (2.0 * math.pi / GRID)
    cosine = jnp.cos(angles)
    sine = jnp.sin(angles)
    return (stacked_table(cosine, -sine), stacked_table(cosine, sine))


def dft_pass(real, imag, table):
    count, size, rest = real.shape
    other = rest // size
    stacked = jnp.concatenate(
        [real.reshape(count, size, size, other), imag.reshape(count, size, size, other)], axis=1
    )
    result = jnp.einsum("ka,mabc->mbck", table, stacked, precision=lax.Precision.HIGHEST)
    out_re = result[..., :size].reshape(count, size, other * size)
    out_im = result[..., size:].reshape(count, size, other * size)
    return (out_re, out_im)


def transform(real, imag, table):
    for _ in range(3):
        real, imag = dft_pass(real, imag, table)
    return (real, imag)


def potential(own_re, own_im, band, kernel, tables):
    band_re = band[0]
    band_im = band[1]
    dens_re = band_re * own_re + band_im * own_im
    dens_im = band_re * own_im - band_im * own_re
    spec_re, spec_im = transform(dens_re, dens_im, tables[0])
    return transform(spec_re * kernel, spec_im * kernel, tables[1])


def both_sides(own_re, own_im, kernel, tables):

    def fold(carry, piece, start):

        def step(index, state):
            band = lax.dynamic_index_in_dim(piece, index, 1, keepdims=False).astype(jnp.float32)
            pot_re, pot_im = potential(own_re, own_im, band, kernel, tables)
            new_re = state[0] + band[0] * pot_re - band[1] * pot_im
            new_im = state[1] + band[0] * pot_im + band[1] * pot_re
            rows_re = jnp.sum(own_re * pot_re + own_im * pot_im, axis=0)
            rows_im = jnp.sum(own_im * pot_re - own_re * pot_im, axis=0)
            rows = jnp.stack([rows_re, rows_im])[:, None]
            back = lax.dynamic_update_slice_in_dim(state[2], rows, index, 1)
            return (new_re, new_im, back)

        return lax.fori_loop(0, piece.shape[1], step, carry)

    return fold


def per_device(psi, kpoint_of_pool):
    own = psi[0]
    band_dev = own.shape[1]
    block = band_dev * lax.axis_size("band")
    pools = lax.axis_size("kpool")
    myself = lax.axis_index("kpool")
    coords = kpoint_coords(kpoint_of_pool)
    here = lax.dynamic_index_in_dim(coords, myself, 0, keepdims=False)
    tables = dft_tables()
    own_re = own[0].astype(jnp.float32)
    own_im = own[1].astype(jnp.float32)
    zeros = jnp.zeros(own_re.shape, jnp.float32)
    total = (zeros, zeros)
    partner = (myself - 1) % pools
    there = lax.dynamic_index_in_dim(coords, partner, 0, keepdims=False)
    fold = both_sides(own_re, own_im, coulomb(here - there), tables)
    arrived = passed_along(own, "kpool", 1)
    empty = jnp.zeros((2, block) + own_re.shape[1:], jnp.float32)
    start_re, start_im, back = fold(
        (total[0], total[1], empty),
        lax.all_gather(arrived, "band", axis=1, tiled=True),
        jnp.int32(0),
    )
    shares = lax.psum_scatter(back, "band", scatter_dimension=1, tiled=True)
    returned = passed_along(shares, "kpool", -1)
    total = (start_re + returned[0], start_im + returned[1])
    weight = -((2.0 * ROUNDS * block) ** (-0.5))
    result = jnp.stack([total[0], total[1]]) * weight
    return result[None]


def solution(mesh):
    in_specs = (P("kpool", None, "band", None, None), P())
    out_specs = P("kpool", None, "band", None, None)
    return jax.shard_map(
        per_device, mesh=mesh, in_specs=in_specs, out_specs=out_specs, check_vma=False
    )
```

profile of v0, /device:TPU:0, one launch (start us, length us, event | category | flops | bytes accessed | tf_op | source)
XLA Modules:
  0.0 378.7 jit_solution(14894622294553525323)
XLA Ops:
  7.0 9.1 %collective-permute-done = bf16[2,1,48,2304]{3,2,1,0:T(8,128)(2,1)S(1)} collective-permute-done((bf16[2,1,48,2304]{3,2,1,0:T(8,128)(2,1)}, bf16[2,1,48,2304]{3,2,1,0:T(8,128)(2,1)S(1)}, u32[]{:S(2)}, u32[]{:S(2)}) %collective-permute-start) | collective-permute-done | bytes 442400 | tf_op jit(solution)/shard_map/ppermute | solution.py:15
  21.0 37.4 %all-gather.2.cloned.1.call-done = bf16[2,4,48,2304]{3,2,1,0:T(8,128)(2,1)} async-done(((bf16[2,1,48,2304]{3,2,1,0:T(8,128)(2,1)}), bf16[2,4,48,2304]{3,2,1,0:T(8,128)(2,1)}) %all-gather.2.cloned.1.call-update) | async-done | bytes 1769488 | tf_op jit(solution)/shard_map/all_gather | solution.py:122
  58.4 165.4 %while.18 = (s32[]{:T(128)}, f32[1,48,2304]{2,1,0:T(8,128)}, f32[1,48,2304]{2,1,0:T(8,128)}, f32[2,4,48,2304]{3,2,1,0:T(8,128)}, bf16[2,4,48,2304]{3,2,1,0:T(8,1...) while((s32[]{:T(128)}, f32[1,48,2304]{2,1,0:T(8,128)}, ...), condition=%wide.region_1.2_spmd.clone, body=%wide.region_0.1_spmd.clone.sunk | while | flops 1533911040 | bytes 61291868 | solution.py:97
  64.2 4.0 %fusion.99 = f32[1,48,48,96]{3,2,1,0:T(8,128)S(1)} fusion(f32[96,48,48]{2,1,0:T(8,128)S(1)} %maximum_bitcast_fusion.15, f32[96,96]{1,0:T(8,128)S(1)} %get-tuple-element.441), kind=kOutput, calls=%fused_computation.17.clone.1 | convolution fusion | flops 254803968 | bytes 1806336 | tf_op jit(solution)/shard_map/while/body/eval_jaxpr/ka,mabc->mbck/dot_general | solution.py:61
  68.8 4.0 %fusion.101 = f32[1,48,48,96]{3,2,1,0:T(8,128)S(1)} fusion(f32[96,48,48]{2,1,0:T(8,128)S(1)} %maximum_bitcast_fusion.16, f32[96,96]{1,0:T(8,128)S(1)} %get-tuple-element.441), kind=kOutput, calls=%fused_computation.18.clone.1 | convolution fusion | flops 254803968 | bytes 1806336 | tf_op jit(solution)/shard_map/while/body/eval_jaxpr/ka,mabc->mbck/dot_general | solution.py:61
  79.7 4.0 %fusion.102 = f32[1,48,48,96]{3,2,1,0:T(8,128)S(1)} fusion(f32[96,48,48]{2,1,0:T(8,128)S(1)} %maximum_bitcast_fusion.17, f32[96,96]{1,0:T(8,128)S(1)} %get-tuple-element.442), kind=kOutput, calls=%fused_computation.19.clone.1 | convolution fusion | flops 254803968 | bytes 1806336 | tf_op jit(solution)/shard_map/while/body/eval_jaxpr/ka,mabc->mbck/dot_general | solution.py:61
  84.3 4.0 %fusion.104 = f32[1,48,48,96]{3,2,1,0:T(8,128)S(1)} fusion(f32[96,48,48]{2,1,0:T(8,128)S(1)} %maximum_bitcast_fusion.18, f32[96,96]{1,0:T(8,128)S(1)} %get-tuple-element.442), kind=kOutput, calls=%fused_computation.20.clone.1 | convolution fusion | flops 254803968 | bytes 1806336 | tf_op jit(solution)/shard_map/while/body/eval_jaxpr/ka,mabc->mbck/dot_general | solution.py:61
  88.8 4.0 %fusion.106 = f32[1,48,48,96]{3,2,1,0:T(8,128)S(1)} fusion(f32[96,48,48]{2,1,0:T(8,128)S(1)} %maximum_bitcast_fusion.19, f32[96,96]{1,0:T(8,128)S(1)} %get-tuple-element.442), kind=kOutput, calls=%fused_computation.21.clone.1 | convolution fusion | flops 254803968 | bytes 1806336 | tf_op jit(solution)/shard_map/while/body/eval_jaxpr/ka,mabc->mbck/dot_general | solution.py:61
  105.4 4.0 %fusion.99 = f32[1,48,48,96]{3,2,1,0:T(8,128)S(1)} fusion(f32[96,48,48]{2,1,0:T(8,128)S(1)} %maximum_bitcast_fusion.15, f32[96,96]{1,0:T(8,128)S(1)} %get-tuple-element.441), kind=kOutput, calls=%fused_computation.17.clone.1 | convolution fusion | flops 254803968 | bytes 1806336 | tf_op jit(solution)/shard_map/while/body/eval_jaxpr/ka,mabc->mbck/dot_general | solution.py:61
  110.0 4.0 %fusion.101 = f32[1,48,48,96]{3,2,1,0:T(8,128)S(1)} fusion(f32[96,48,48]{2,1,0:T(8,128)S(1)} %maximum_bitcast_fusion.16, f32[96,96]{1,0:T(8,128)S(1)} %get-tuple-element.441), kind=kOutput, calls=%fused_computation.18.clone.1 | convolution fusion | flops 254803968 | bytes 1806336 | tf_op jit(solution)/shard_map/while/body/eval_jaxpr/ka,mabc->mbck/dot_general | solution.py:61
  120.9 4.0 %fusion.102 = f32[1,48,48,96]{3,2,1,0:T(8,128)S(1)} fusion(f32[96,48,48]{2,1,0:T(8,128)S(1)} %maximum_bitcast_fusion.17, f32[96,96]{1,0:T(8,128)S(1)} %get-tuple-element.442), kind=kOutput, calls=%fused_computation.19.clone.1 | convolution fusion | flops 254803968 | bytes 1806336 | tf_op jit(solution)/shard_map/while/body/eval_jaxpr/ka,mabc->mbck/dot_general | solution.py:61
  125.5 4.0 %fusion.104 = f32[1,48,48,96]{3,2,1,0:T(8,128)S(1)} fusion(f32[96,48,48]{2,1,0:T(8,128)S(1)} %maximum_bitcast_fusion.18, f32[96,96]{1,0:T(8,128)S(1)} %get-tuple-element.442), kind=kOutput, calls=%fused_computation.20.clone.1 | convolution fusion | flops 254803968 | bytes 1806336 | tf_op jit(solution)/shard_map/while/body/eval_jaxpr/ka,mabc->mbck/dot_general | solution.py:61
  130.1 4.0 %fusion.106 = f32[1,48,48,96]{3,2,1,0:T(8,128)S(1)} fusion(f32[96,48,48]{2,1,0:T(8,128)S(1)} %maximum_bitcast_fusion.19, f32[96,96]{1,0:T(8,128)S(1)} %get-tuple-element.442), kind=kOutput, calls=%fused_computation.21.clone.1 | convolution fusion | flops 254803968 | bytes 1806336 | tf_op jit(solution)/shard_map/while/body/eval_jaxpr/ka,mabc->mbck/dot_general | solution.py:61
  146.8 4.0 %fusion.99 = f32[1,48,48,96]{3,2,1,0:T(8,128)S(1)} fusion(f32[96,48,48]{2,1,0:T(8,128)S(1)} %maximum_bitcast_fusion.15, f32[96,96]{1,0:T(8,128)S(1)} %get-tuple-element.441), kind=kOutput, calls=%fused_computation.17.clone.1 | convolution fusion | flops 254803968 | bytes 1806336 | tf_op jit(solution)/shard_map/while/body/eval_jaxpr/ka,mabc->mbck/dot_general | solution.py:61
  151.4 4.0 %fusion.101 = f32[1,48,48,96]{3,2,1,0:T(8,128)S(1)} fusion(f32[96,48,48]{2,1,0:T(8,128)S(1)} %maximum_bitcast_fusion.16, f32[96,96]{1,0:T(8,128)S(1)} %get-tuple-element.441), kind=kOutput, calls=%fused_computation.18.clone.1 | convolution fusion | flops 254803968 | bytes 1806336 | tf_op jit(solution)/shard_map/while/body/eval_jaxpr/ka,mabc->mbck/dot_general | solution.py:61
  162.3 4.0 %fusion.102 = f32[1,48,48,96]{3,2,1,0:T(8,128)S(1)} fusion(f32[96,48,48]{2,1,0:T(8,128)S(1)} %maximum_bitcast_fusion.17, f32[96,96]{1,0:T(8,128)S(1)} %get-tuple-element.442), kind=kOutput, calls=%fused_computation.19.clone.1 | convolution fusion | flops 254803968 | bytes 1806336 | tf_op jit(solution)/shard_map/while/body/eval_jaxpr/ka,mabc->mbck/dot_general | solution.py:61
  166.9 4.0 %fusion.104 = f32[1,48,48,96]{3,2,1,0:T(8,128)S(1)} fusion(f32[96,48,48]{2,1,0:T(8,128)S(1)} %maximum_bitcast_fusion.18, f32[96,96]{1,0:T(8,128)S(1)} %get-tuple-element.442), kind=kOutput, calls=%fused_computation.20.clone.1 | convolution fusion | flops 254803968 | bytes 1806336 | tf_op jit(solution)/shard_map/while/body/eval_jaxpr/ka,mabc->mbck/dot_general | solution.py:61
  171.5 4.0 %fusion.106 = f32[1,48,48,96]{3,2,1,0:T(8,128)S(1)} fusion(f32[96,48,48]{2,1,0:T(8,128)S(1)} %maximum_bitcast_fusion.19, f32[96,96]{1,0:T(8,128)S(1)} %get-tuple-element.442), kind=kOutput, calls=%fused_computation.21.clone.1 | convolution fusion | flops 254803968 | bytes 1806336 | tf_op jit(solution)/shard_map/while/body/eval_jaxpr/ka,mabc->mbck/dot_general | solution.py:61
  188.2 4.0 %fusion.99 = f32[1,48,48,96]{3,2,1,0:T(8,128)S(1)} fusion(f32[96,48,48]{2,1,0:T(8,128)S(1)} %maximum_bitcast_fusion.15, f32[96,96]{1,0:T(8,128)S(1)} %get-tuple-element.441), kind=kOutput, calls=%fused_computation.17.clone.1 | convolution fusion | flops 254803968 | bytes 1806336 | tf_op jit(solution)/shard_map/while/body/eval_jaxpr/ka,mabc->mbck/dot_general | solution.py:61
  203.6 4.0 %fusion.102 = f32[1,48,48,96]{3,2,1,0:T(8,128)S(1)} fusion(f32[96,48,48]{2,1,0:T(8,128)S(1)} %maximum_bitcast_fusion.17, f32[96,96]{1,0:T(8,128)S(1)} %get-tuple-element.442), kind=kOutput, calls=%fused_computation.19.clone.1 | convolution fusion | flops 254803968 | bytes 1806336 | tf_op jit(solution)/shard_map/while/body/eval_jaxpr/ka,mabc->mbck/dot_general | solution.py:61
  208.2 4.0 %fusion.104 = f32[1,48,48,96]{3,2,1,0:T(8,128)S(1)} fusion(f32[96,48,48]{2,1,0:T(8,128)S(1)} %maximum_bitcast_fusion.18, f32[96,96]{1,0:T(8,128)S(1)} %get-tuple-element.442), kind=kOutput, calls=%fused_computation.20.clone.1 | convolution fusion | flops 254803968 | bytes 1806336 | tf_op jit(solution)/shard_map/while/body/eval_jaxpr/ka,mabc->mbck/dot_general | solution.py:61
  212.8 4.0 %fusion.106 = f32[1,48,48,96]{3,2,1,0:T(8,128)S(1)} fusion(f32[96,48,48]{2,1,0:T(8,128)S(1)} %maximum_bitcast_fusion.19, f32[96,96]{1,0:T(8,128)S(1)} %get-tuple-element.442), kind=kOutput, calls=%fused_computation.21.clone.1 | convolution fusion | flops 254803968 | bytes 1806336 | tf_op jit(solution)/shard_map/while/body/eval_jaxpr/ka,mabc->mbck/dot_general | solution.py:61
  225.1 131.5 %all-reduce.3.cloned.1.call-done = f32[2,4,48,2304]{3,2,1,0:T(8,128)} async-done(((f32[2,4,48,2304]{3,2,1,0:T(8,128)}), f32[2,4,48,2304]{3,2,1,0:T(8,128)}) %all-reduce.3.cloned.1.call-update) | async-done | bytes 3538960
  360.2 10.6 %collective-permute-done.1 = f32[2,1,48,2304]{3,2,1,0:T(8,128)S(1)} collective-permute-done((f32[2,1,48,2304]{3,2,1,0:T(8,128)S(1)}, f32[2,1,48,2304]{3,2,1,0:T(8,128)S(1)}, u32[]{:S(2)}, u32[]{:S(2)}) %collective-permute-start.1) | collective-permute-done | bytes 884768 | tf_op jit(solution)/shard_map/ppermute | solution.py:15
  (201 shorter events, 99.2 us)
Async XLA Ops:
  6.5 14.4 %copy-start.10 = (bf16[1,2,1,48,2304]{4,3,2,1,0:T(8,128)(2,1)S(1)}, bf16[1,2,1,48,2304]{4,3,2,1,0:T(8,128)(2,1)}, u32[]{:S(2)}) copy-start(bf16[1,2,1,48,2304]{4,3,2,1,0:T(8,128)(2,1)} %param.4) | copy-start | bytes 1327108
  6.5 51.9 %all-gather.2.cloned.1.call-start = ((), (), s32[]{:S(2)}) async-start(), calls=%async_computation | async-start | bytes 2211840 | tf_op jit(solution)/shard_map/all_gather | solution.py:122
  6.5 9.6 %collective-permute-start = (bf16[2,1,48,2304]{3,2,1,0:T(8,128)(2,1)}, bf16[2,1,48,2304]{3,2,1,0:T(8,128)(2,1)S(1)}, u32[]{:S(2)}, u32[]{:S(2)}) collective-permute-start(bf16[2,1,48,2304]{3,2,1,0:T(8,128)(2,1)} %bitcast.154), channel_id=1, source_target_pairs={{0,4},{4,8},{8,12},{12,16},{16,20},{20,24},{24,28},{28,0},{1,5},{5... | collective-permute-start | bytes 1327112 | tf_op jit(solution)/shard_map/ppermute | solution.py:15
  17.0 339.6 %all-reduce.3.cloned.1.call-start = ((), (), s32[]{:S(2)}) async-start(), calls=%async_computation.1 | async-start | bytes 7077888
  58.4 2.3 copy-start
  58.4 2.3 copy-start.2
  94.5 1.1 copy-start.5
  98.0 1.3 copy-start.1
  98.0 1.6 copy-start.3
  99.7 2.3 copy-start
  99.7 2.3 copy-start.2
  139.4 1.3 copy-start.1
  139.4 1.6 copy-start.3
  141.0 2.3 copy-start
  141.0 2.3 copy-start.2
  180.8 1.3 copy-start.1
  180.8 1.6 copy-start.3
  182.4 2.3 copy-start
  182.4 2.3 copy-start.2
  222.1 1.3 copy-start.1
  222.1 1.6 copy-start.3
  223.8 147.0 %copy-start.7 = (f32[1,48,2304]{2,1,0:T(8,128)S(1)}, f32[1,48,2304]{2,1,0:T(8,128)}, u32[]{:S(2)}) copy-start(f32[1,48,2304]{2,1,0:T(8,128)} %get-tuple-element.176) | copy-start | bytes 1327108
  223.8 146.9 %copy-start.8 = (f32[1,48,2304]{2,1,0:T(8,128)S(1)}, f32[1,48,2304]{2,1,0:T(8,128)}, u32[]{:S(2)}) copy-start(f32[1,48,2304]{2,1,0:T(8,128)} %get-tuple-element.178) | copy-start | bytes 1327108
  358.5 12.3 %collective-permute-start.1 = (f32[2,1,48,2304]{3,2,1,0:T(8,128)S(1)}, f32[2,1,48,2304]{3,2,1,0:T(8,128)S(1)}, u32[]{:S(2)}, u32[]{:S(2)}) collective-permute-start(f32[2,1,48,2304]{3,2,1,0:T(8,128)S(1)} %constant_dynamic-slice_fusion), channel_id=1, source_target_pairs={{0,28},{4,0},{8,4},{12,8},{16,12},{20,16},{24,20},{28,24},{1,29},{... | collective-permute-start | bytes 2654216 | tf_op jit(solution)/shard_map/ppermute | solution.py:15
  (13 other events, 13.1 us)
Sparse Core Ops, SparseCore 0:
  17.1 41.2 all-gather.1
  223.9 132.6 all-reduce.2
where the time goes:
time: 380 us; the launch traced here: 379 us
  waiting for transfers between devices  189 us (50%)
  matrix products  85.6 us (23%)
  local copies, waits for them, and re-layouts  48.8 us (13%)
  other arithmetic  39.3 us (10%)
  between operations  13.5 us (4%)
    unnamed x3, waiting for transfers between devices  132 us
    dot_general x24, matrix products, dft_pass(): jnp.einsum('ka,mabc->mbck', table, stacked, precision=lax.Precision.HIGHEST)  85.6 us
    all_gather x1, waiting for transfers between devices, per_device(): lax.all_gather(arrived, 'band', axis=1, tiled=True)  37.4 us
    ppermute x2, waiting for transfers between devices, passed_along(): lax.ppermute(value, axis, [(i, (i + by) % size) for i in range(size)])  19.7 us
    add x4, other arithmetic, step(): rows_re = jnp.sum(own_re * pot_re + own_im * pot_im, axis=0)  9.83 us
    div x4, other arithmetic, coulomb(): return kernel.reshape(GRID, GRID * GRID) / (GRID * GRID * GRID)  7.69 us
  transfers between devices with their start and end apart: 4, of which 4 were waited for; matrix products, arithmetic and copies ran while one was open for 1% of the time, Pallas kernels for 0%

commit v1 on v0

v1 whole, which is shorter than its diff:
```python
import functools
import math

import jax
import jax.numpy as jnp
import numpy as np
from jax import lax
from jax.experimental import pallas as pl
from jax.experimental.pallas import tpu as pltpu
from jax.sharding import PartitionSpec as P

KMESH = 4
ROUNDS = 1


def passed_along(value, axis, by):
    size = lax.axis_size(axis)
    return lax.ppermute(value, axis, [(i, (i + by) % size) for i in range(size)])


def kpoint_coords(labels):
    first = labels % KMESH
    second = labels // KMESH % KMESH
    third = labels // (KMESH * KMESH)
    return jnp.stack([first, second, third], axis=1).astype(jnp.float32) / KMESH


def half_width(grid):
    return -(-grid // 64) * 64


def coulomb(offset, grid):
    half = half_width(grid)
    index = jnp.arange(grid, dtype=jnp.int32)
    lane = jnp.arange(2 * half, dtype=jnp.int32) % half

    def freq(i):
        return jnp.where(i < grid // 2, i, i - grid).astype(jnp.float32)

    edge = index == grid // 2
    edge_z = (lane == grid // 2) | (lane >= grid)
    along_x = (offset[0] + freq(index)) ** 2
    along_y = (offset[1] + freq(index)) ** 2
    along_z = (offset[2] + freq(lane)) ** 2
    squared = along_x[None, :, None] + along_y[:, None, None] + along_z[None, None, :]
    cutoff = edge[None, :, None] | edge[:, None, None] | edge_z[None, None, :]
    safe = jnp.where(cutoff, 1.0, squared)
    amplitude = grid**1.5 / 16.0
    return jnp.where(cutoff, 0.0, amplitude / safe) / (grid * grid * grid)


def two_parts(table):
    high = table.astype(jnp.bfloat16)
    low = (table - high.astype(np.float32)).astype(jnp.bfloat16)
    return high, low


def dft_tables(grid):
    half = half_width(grid)
    index = np.arange(grid)
    angles = (index[:, None] * index[None, :] % grid) * (2.0 * math.pi / grid)
    cosine = np.cos(angles).astype(np.float32)
    sine = np.sin(angles).astype(np.float32)
    lanes = []
    for sign in (1.0, -1.0):
        full = np.zeros((2 * half, 2 * half), np.float32)
        full[:grid, :grid] = cosine
        full[half : half + grid, half : half + grid] = cosine
        full[:grid, half : half + grid] = -sign * sine
        full[half : half + grid, :grid] = sign * sine
        high, low = two_parts(full)
        lanes.append(np.block([[high, low], [high, np.zeros_like(low)]]))
    high, low = two_parts(np.concatenate([cosine, sine], axis=0))
    rows = np.concatenate([high, high, low], axis=1)
    return np.stack(lanes), rows


def split(x):
    high = x.astype(jnp.bfloat16)
    low = (x - high.astype(jnp.float32)).astype(jnp.bfloat16)
    return high, low


def kernel(grid, batch, own_ref, band_ref, v_ref, lanes_ref, rows_ref, acc_ref, back_ref, field):
    half = half_width(grid)
    width = 2 * half
    first = lax.broadcasted_iota(jnp.int32, (1, width), 1) < half
    sign = jnp.where(first, 1.0, -1.0).astype(jnp.float32)

    def swap(x):
        return pltpu.roll(x, half, 1)

    def turned(x):
        return swap(x) * sign

    def both(x):
        other = swap(x)
        return jnp.where(first, x, other), jnp.where(first, other, x)

    def along_lanes(x, which):
        high, low = split(x)
        out = jnp.dot(
            jnp.concatenate([high, low], axis=1),
            lanes_ref[which],
            preferred_element_type=jnp.float32,
        )
        return out[:, :width] + out[:, width:]

    def along_rows(xs, sense):
        parts = []
        for x in xs:
            high, low = split(x)
            parts.append(jnp.concatenate([high, low, high], axis=0))
        outs = []
        for at in range(0, len(parts), 2):
            pair = jnp.concatenate(parts[at : at + 2], axis=1)
            out = jnp.dot(rows_ref[...], pair, preferred_element_type=jnp.float32)
            for j in range(len(parts[at : at + 2])):
                piece = out[:, j * width : (j + 1) * width]
                q = turned(piece[grid:])
                outs.append(piece[:grid] + q if sense > 0 else piece[:grid] - q)
        return outs

    def rows_of(step):
        return pl.ds(pl.multiple_of(step * (batch * grid), batch * grid), batch * grid)

    def forward(step, carry):
        rows = rows_of(step)
        own = own_ref[rows, :].astype(jnp.float32)
        b_re, b_im = both(band_ref[0, rows, :].astype(jnp.float32))
        dens = b_re * own + b_im * turned(own)
        spec = along_lanes(dens, 0)
        outs = along_rows([spec[j * grid : (j + 1) * grid] for j in range(batch)], 1)
        field[rows, :] = jnp.concatenate(outs, axis=0)
        return carry

    lax.fori_loop(0, grid // batch, forward, 0)

    def middle(step, carry):
        at = step * batch
        xs = [field[pl.ds(at + j, grid, stride=grid), :] for j in range(batch)]
        spec = along_rows(xs, 1)
        spec = [spec[j] * v_ref[at + j] for j in range(batch)]
        outs = along_rows(spec, -1)
        for j in range(batch):
            field[pl.ds(at + j, grid, stride=grid), :] = outs[j]
        return carry

    lax.fori_loop(0, grid // batch, middle, 0)

    fresh = pl.program_id(0) == 0

    def backward(step, carry):
        rows = rows_of(step)
        mid = field[rows, :]
        outs = along_rows([mid[j * grid : (j + 1) * grid] for j in range(batch)], -1)
        pot = along_lanes(jnp.concatenate(outs, axis=0), 1)
        own = own_ref[rows, :].astype(jnp.float32)
        b_re, b_im = both(band_ref[0, rows, :].astype(jnp.float32))
        w_re, w_im = both(pot)
        back_ref[0, rows, :] = w_re * own + w_im * turned(own)
        new = b_re * pot - b_im * turned(pot)
        acc_ref[rows, :] = jnp.where(fresh, new, acc_ref[rows, :] + new)
        return carry

    lax.fori_loop(0, grid // batch, backward, 0)


def pair_sums(own, bands, v, grid, batch=8):
    count = bands.shape[0]
    points, width = own.shape
    lanes, rows = dft_tables(grid)
    whole = pl.BlockSpec(memory_space=pltpu.VMEM)
    return pl.pallas_call(
        functools.partial(kernel, grid, batch),
        grid=(count,),
        in_specs=[
            whole,
            pl.BlockSpec((1, points, width), lambda m: (m, 0, 0)),
            whole,
            whole,
            whole,
        ],
        out_specs=[
            pl.BlockSpec((points, width), lambda m: (0, 0)),
            pl.BlockSpec((1, points, width), lambda m: (m, 0, 0)),
        ],
        out_shape=[
            jax.ShapeDtypeStruct((points, width), jnp.float32),
            jax.ShapeDtypeStruct((count, points, width), jnp.float32),
        ],
        scratch_shapes=[pltpu.VMEM((points, width), jnp.float32)],
        compiler_params=pltpu.CompilerParams(dimension_semantics=("arbitrary",)),
    )(own, bands, v, jnp.asarray(lanes), jnp.asarray(rows))


def per_device(psi, kpoint_of_pool):
    own = psi[0]
    grid = own.shape[2]
    half = half_width(grid)
    band_dev = own.shape[1]
    block = band_dev * lax.axis_size("band")
    pools = lax.axis_size("kpool")
    myself = lax.axis_index("kpool")
    coords = kpoint_coords(kpoint_of_pool)
    here = lax.dynamic_index_in_dim(coords, myself, 0, keepdims=False)
    there = lax.dynamic_index_in_dim(coords, (myself - 1) % pools, 0, keepdims=False)
    v = coulomb(here - there, grid)
    points = grid * grid
    parts = own.reshape(2, band_dev, points, grid)
    parts = jnp.pad(parts, ((0, 0), (0, 0), (0, 0), (0, half - grid)))
    packed = jnp.concatenate([parts[0], parts[1]], axis=-1)
    arrived = passed_along(packed, "kpool", 1)
    bands = lax.all_gather(arrived, "band", axis=0, tiled=True)
    accs, back = [], None
    for n in range(band_dev):
        acc, rows = pair_sums(packed[n], bands, v, grid)
        accs.append(acc)
        back = rows if back is None else back + rows
    shares = lax.psum_scatter(back, "band", scatter_dimension=0, tiled=True)
    returned = passed_along(shares, "kpool", -1)
    weight = -((2.0 * ROUNDS * block) ** (-0.5))
    total = (jnp.stack(accs) + returned) * weight
    result = jnp.stack([total[..., :grid], total[..., half : half + grid]])
    return result.reshape(2, band_dev, grid, grid * grid)[None]


def solution(mesh):
    in_specs = (P("kpool", None, "band", None, None), P())
    out_specs = P("kpool", None, "band", None, None)
    return jax.shard_map(
        per_device, mesh=mesh, in_specs=in_specs, out_specs=out_specs, check_vma=False
    )
```

time: 380 us -> 225 us (0.59)
  matrix products: 85.6 us -> 0 us
  local copies, waits for them, and re-layouts: 48.8 us -> 5.68 us
  Pallas kernels: 0 us -> 42.7 us
  waiting for transfers between devices: 189 us -> 154 us
  other arithmetic: 39.3 us -> 6.88 us
    unnamed x3 -> x2, waiting for transfers between devices: 132 us -> 0.03 us
    dot_general x24 -> x0, matrix products: 85.6 us -> none  [dft_pass(): jnp.einsum('ka,mabc->mbck', table, stacked, precision=lax.Precision.HIGHEST)]
    reduce_scatter x0 -> x1, waiting for transfers between devices: none -> 84.2 us  [per_device(): shares = lax.psum_scatter(back, 'band', scatter_dimension=0, tiled=True)]
    pallas_call x0 -> x1, Pallas kernels: none -> 42.7 us  [pair_sums(): pl.pallas_call(functools.partial(kernel, grid, batch), grid=(count,), in_...]
    add x9 -> x1, other arithmetic: 13.4 us -> 0.07 us  [coulomb(): along_x[None, :, None] + along_y[:, None, None] + along_z[None, None, :]]
    add x14 -> x0, local copies, waits for them, and re-layouts: 12 us -> none  [the longest x10 6.5 us: coulomb(): along_x[:, None, None] + along_y[None, :, None] + along_z[None, None, :]]
    all_gather x1, waiting for transfers between devices: 37.4 us -> 45.1 us  [per_device(): bands = lax.all_gather(arrived, 'band', axis=0, tiled=True)]
    slice x21 -> x2, local copies, waits for them, and re-layouts: 8.06 us -> 0.96 us  [the longest x1 0.59 us: coulomb(): along_x = (offset[0] + freq(index)) ** 2]
  transfers between devices with their start and end apart: 4 -> 4, of which waited for: 4 -> 4; matrix products, arithmetic and copies ran while one was open for 1% -> 3% of each run, Pallas kernels for 0% -> 0%
where the time goes in v1:
time: 225 us
  waiting for transfers between devices  154 us (68%)
  Pallas kernels  42.7 us (19%)
  between operations  13.5 us (6%)
  other arithmetic  6.88 us (3%)
  local copies, waits for them, and re-layouts  5.68 us (3%)
  starting transfers between devices  2.36 us (1%)
    reduce_scatter x1, waiting for transfers between devices, per_device(): shares = lax.psum_scatter(back, 'band', scatter_dimension=0, tiled=True)  84.2 us
    all_gather x1, waiting for transfers between devices, per_device(): bands = lax.all_gather(arrived, 'band', axis=0, tiled=True)  45.1 us
    pallas_call x1, Pallas kernels, pair_sums(): pl.pallas_call(functools.partial(kernel, grid, batch), grid=(count,), in_...  42.7 us
    ppermute x2, waiting for transfers between devices, passed_along(): lax.ppermute(value, axis, [(i, (i + by) % size) for i in range(size)])  24.5 us
  transfers between devices with their start and end apart: 4, of which 4 were waited for; matrix products, arithmetic and copies ran while one was open for 3% of the time, Pallas kernels for 0%

profile of v1, /device:TPU:0, one launch (start us, length us, event | category | flops | bytes accessed | tf_op | source)
XLA Modules:
  0.0 225.0 jit_solution(13993299062700749717)
XLA Ops:
  6.5 2.6 %reshape_squeeze.3 = bf16[2,1,2304,48]{3,2,0,1:T(8,128)(2,1)S(1)} reshape(bf16[1,2,1,48,2304]{4,3,2,1,0:T(8,128)(2,1)} %param.4) | data formatting | bytes 884736 | tf_op jit(solution)/shard_map/reshape;squeeze | solution.py:210
  9.2 0.2 fusion.3
  9.4 0.3 pad_maximum_fusion.1
  9.8 0.5 collective-permute-start
  10.3 10.4 %collective-permute-done = bf16[1,2304,128]{2,1,0:T(8,128)(2,1)S(1)} collective-permute-done((bf16[1,2304,128]{2,1,0:T(8,128)(2,1)S(1)}, bf16[1,2304,128]{2,1,0:T(8,128)(2,1)S(1)}, u32[]{:S(2)}, u32[]{:S(2)}) %collective-permute-start) | collective-permute-done | bytes 589856 | tf_op jit(solution)/shard_map/ppermute | solution.py:18
  20.8 0.8 copy-done.1
  21.8 0.1 dynamic-slice_subtract_fusion
  21.8 0.6 fusion.15
  22.4 0.6 fusion.12
  23.1 1.3 add_multiply_fusion
  24.3 0.1 broadcast_or_fusion
  24.4 0.1 broadcast_add_fusion
  24.5 2.1 fusion.1.v_ref
  26.6 1.1 fusion.16.own_ref
  27.8 45.1 %all-gather.2.cloned.1.call-done.band_ref = bf16[4,2304,128]{2,1,0:T(8,128)(2,1)} async-done(((bf16[1,2304,128]{2,1,0:T(8,128)(2,1)}), bf16[4,2304,128]{2,1,0:T(8,128)(2,1)}) %all-gather.2.cloned.1.call-update) | async-done | bytes 2359312 | tf_op jit(solution)/shard_map/all_gather | solution.py:214
  72.8 42.7 %shard_map.46 = (f32[2304,128]{1,0:T(8,128)}, f32[4,2304,128]{2,1,0:T(8,128)}) custom-call(bf16[2304,128]{1,0:T(8,128)(2,1)} %fusion.16.own_ref, bf16[4,2304,128]{2,1,0:T(8,128)(2,1)} %all-gather.2.cloned.1.call-done.band_ref, f32[48,48,128]{2,1,0:T(8,128)} %fusion.1.v_ref, bf16[2,256,256]{2,1,0:T(8,128)(2,1)} %constant.114.clone.lanes_ref, ...), custom_call_target="tpu_custom_call" | custom-call | tf_op jit(solution)/shard_map/pallas_call | solution.py:174
  115.6 84.2 %reduce-scatter.2.cloned.1.call-done = f32[1,2304,128]{2,1,0:T(8,128)} async-done(((f32[4,2304,128]{2,1,0:T(8,128)}), f32[1,2304,128]{2,1,0:T(8,128)}) %reduce-scatter.2.cloned.1.call-update) | async-done | bytes 1179664 | tf_op jit(solution)/shard_map/reduce_scatter | solution.py:220
  199.8 1.8 collective-permute-start.1
  201.6 14.0 %collective-permute-done.1 = f32[1,2304,128]{2,1,0:T(8,128)S(1)} collective-permute-done((f32[1,2304,128]{2,1,0:T(8,128)}, f32[1,2304,128]{2,1,0:T(8,128)S(1)}, u32[]{:S(2)}, u32[]{:S(2)}) %collective-permute-start.1) | collective-permute-done | bytes 1179680 | tf_op jit(solution)/shard_map/ppermute | solution.py:18
  215.6 0.1 fusion.2
  215.8 0.4 fusion.14
  216.1 0.5 stack.29
  216.7 0.5 stack.30
  217.2 1.0 pad_maximum_fusion
  (13 shorter events, 0.1 us)
Async XLA Ops:
  6.5 66.3 %all-gather.2.cloned.1.call-start = ((), (), s32[]{:S(2)}) async-start(), calls=%async_computation.1 | async-start | bytes 2949120 | tf_op jit(solution)/shard_map/all_gather | solution.py:214
  9.4 12.3 %copy-start.2 = (s32[8]{0:T(128)S(1)}, s32[8]{0:T(128)}, u32[]{:S(2)}) copy-start(s32[8]{0:T(128)} %param.5) | copy-start | bytes 100
  9.8 11.0 %collective-permute-start = (bf16[1,2304,128]{2,1,0:T(8,128)(2,1)S(1)}, bf16[1,2304,128]{2,1,0:T(8,128)(2,1)S(1)}, u32[]{:S(2)}, u32[]{:S(2)}) collective-permute-start(bf16[1,2304,128]{2,1,0:T(8,128)(2,1)S(1)} %pad_maximum_fusion.1), channel_id=1, source_target_pairs={{0,4},{4,8},{8,12},{12,16},{16,20},{20,24},{24,28},{28,0},{1,5},{5... | collective-permute-start | bytes 1769480 | tf_op jit(solution)/shard_map/ppermute | solution.py:18
  20.8 0.8 copy-start.1
  21.6 178.2 %reduce-scatter.2.cloned.1.call-start = ((), (), s32[]{:S(2)}) async-start(), calls=%async_computation.2 | async-start | bytes 5898240 | tf_op jit(solution)/shard_map/reduce_scatter | solution.py:220
  115.6 100.0 %copy-start = (f32[2304,128]{1,0:T(8,128)S(1)}, f32[2304,128]{1,0:T(8,128)}, u32[]{:S(2)}) copy-start(f32[2304,128]{1,0:T(8,128)} %get-tuple-element.7) | copy-start | bytes 3538948
  199.8 15.8 %collective-permute-start.1 = (f32[1,2304,128]{2,1,0:T(8,128)}, f32[1,2304,128]{2,1,0:T(8,128)S(1)}, u32[]{:S(2)}, u32[]{:S(2)}) collective-permute-start(f32[1,2304,128]{2,1,0:T(8,128)} %reduce-scatter.2.cloned.1.call-done), channel_id=1, source_target_pairs={{0,28},{4,0},{8,4},{12,8},{16,12},{20,16},{24,20},{28,24},{1,29},{... | collective-permute-start | bytes 3538952 | tf_op jit(solution)/shard_map/ppermute | solution.py:18
Sparse Core Ops, SparseCore 0:
  21.7 51.0 all-gather.1
  115.7 84.0 reduce-scatter.1
